TPU v7x, 32 devices: a whole 2x2x4 slice. The times are simulated.
32 devices in a mesh: lon: 8 (over z, core), head: 4 (over y, x).
Axes of the slice: x: 2, y: 2, z: 4, core: 2. Of those that a mesh axis runs over, the one named last changes fastest.
Arguments:
- image_tokens: bfloat16 [64, 128, 3072], P(None, 'lon'), may hold values from -6 to 6
- conditioning: bfloat16 [3072], replicated, may hold values from -6 to 6
- mod_weight: bfloat16 [3072, 3, 3072], P(('lon', 'head')), may hold values from -0.21875 to 0.21875
- mod_bias: bfloat16 [3, 3072], replicated, may hold values from -3 to 3
- qkv_weight: bfloat16 [3072, 3, 3072], P('lon', None, 'head'), may hold values from -0.109375 to 0.109375
- qkv_bias: bfloat16 [3, 3072], P(None, 'head'), may hold values from -3 to 3
- q_gain: float32 [128], replicated, may hold values from 0.5 to 12
- k_gain: float32 [128], replicated, may hold values from 0.5 to 12
- text_kv: bfloat16 [2, 512, 3072], P(None, 'lon', 'head'), may hold values from -6 to 6
- proj_weight: bfloat16 [3072, 3072], P('lon', 'head'), may hold values from -0.109375 to 0.109375
- proj_bias: bfloat16 [3072], replicated, may hold values from -3 to 3
Outputs:
- block_output: bfloat16 [64, 128, 3072], P(None, 'lon', 'head')
All inputs are finite; a program needn't handle non-finite values.
Results may differ from a plain program's by a relative error of at most 0.0109.
The roundings to bfloat16 on the way count: a program that leaves them out, or rounds other values in their place, can miss the bound.
Values may be sent and summed in bfloat16 or wider, within the bound.
A program may use at most 128 MiB of HBM per device.

v0:
```python
import math
import jax
import jax.numpy as jnp
from jax import lax
from jax.sharding import PartitionSpec as P

RADIUS = 15
QROWS = 16


def padded_2(cells, sides, width):
    for axis, dim in sides:
        count = lax.axis_size(axis)
        head = lax.slice_in_dim(cells, 0, width, axis=dim)
        tail = lax.slice_in_dim(cells, cells.shape[dim] - width, cells.shape[dim], axis=dim)
        cells = jnp.concatenate(
            [
                lax.ppermute(tail, axis, [(i, (i + 1) % count) for i in range(count)]),
                cells,
                lax.ppermute(head, axis, [((i + 1) % count, i) for i in range(count)]),
            ],
            axis=dim,
        )
    return cells


def rms_scale(entries, gain):
    mean_square = jnp.mean(entries * entries, axis=-1, keepdims=True)
    return entries * lax.rsqrt(mean_square + 1e-06) * gain


def window_mask(row_first, q_rows, q_cols, k_rows, k_cols, lat_total):
    query_index = jnp.arange(q_rows * q_cols, dtype=jnp.int32)
    key_index = jnp.arange(k_rows * k_cols, dtype=jnp.int32)
    query_row = (query_index // q_cols)[:, None]
    query_col = (query_index % q_cols)[:, None]
    key_row = (key_index // k_cols)[None, :]
    key_col = (key_index % k_cols)[None, :]
    global_row = row_first + key_row - RADIUS
    near_rows = jnp.abs(key_row - RADIUS - query_row) <= RADIUS
    near_cols = jnp.abs(key_col - RADIUS - query_col) <= RADIUS
    inside = (global_row >= 0) & (global_row < lat_total)
    return near_rows & near_cols & inside


def attend(queries, key_block, value_block, text_keys, text_values, row_first, lat_total):
    q_rows, q_cols, heads_here, head_dim = queries.shape
    k_rows, k_cols = (key_block.shape[0], key_block.shape[1])
    flat_query = queries.reshape(q_rows * q_cols, heads_here, head_dim)
    flat_keys = key_block.reshape(k_rows * k_cols, heads_here, head_dim)
    flat_values = value_block.reshape(k_rows * k_cols, heads_here, head_dim)
    factor = 1.0 / math.sqrt(head_dim)
    image_scores = (
        jnp.einsum("qhd,khd->hqk", flat_query, flat_keys, preferred_element_type=jnp.float32)
        * factor
    )
    text_scores = (
        jnp.einsum("qhd,khd->hqk", flat_query, text_keys, preferred_element_type=jnp.float32)
        * factor
    )
    allowed = window_mask(row_first, q_rows, q_cols, k_rows, k_cols, lat_total)
    image_scores = jnp.where(allowed[None], image_scores, -jnp.inf)
    highest = jnp.maximum(
        jnp.max(image_scores, axis=2, keepdims=True), jnp.max(text_scores, axis=2, keepdims=True)
    )
    image_exp = jnp.exp(image_scores - highest)
    text_exp = jnp.exp(text_scores - highest)
    normaliser = jnp.sum(image_exp, axis=2, keepdims=True) + jnp.sum(
        text_exp, axis=2, keepdims=True
    )
    image_probs = (image_exp / normaliser).astype(jnp.bfloat16)
    text_probs = (text_exp / normaliser).astype(jnp.bfloat16)
    combined = jnp.einsum(
        "hqk,khd->qhd", image_probs, flat_values, preferred_element_type=jnp.float32
    )
    combined = combined + jnp.einsum(
        "hqk,khd->qhd", text_probs, text_values, preferred_element_type=jnp.float32
    )
    return combined.astype(jnp.bfloat16).reshape(q_rows, q_cols, heads_here * head_dim)


def body(
    image_tokens,
    conditioning,
    mod_weight,
    mod_bias,
    qkv_weight,
    qkv_bias,
    q_gain,
    k_gain,
    text_kv,
    proj_weight,
    proj_bias,
):
    lat_rows, col_count, model_width = image_tokens.shape
    token_count = lat_rows * col_count
    head_groups = lax.axis_size("head")
    slice_rows = mod_weight.shape[0]
    row_offset = (lax.axis_index("lon") * head_groups + lax.axis_index("head")) * slice_rows
    silu_part = jax.nn.silu(
        lax.dynamic_slice_in_dim(conditioning, row_offset, slice_rows, 0).astype(jnp.float32)
    )
    partial_mod = jnp.dot(
        silu_part,
        mod_weight.reshape(slice_rows, 3 * model_width).astype(jnp.float32),
        precision=lax.Precision.HIGHEST,
    )
    modulation = lax.psum(partial_mod, ("lon", "head")).reshape(3, model_width) + mod_bias.astype(
        jnp.float32
    )
    token_values = image_tokens.reshape(token_count, model_width).astype(jnp.float32)
    average = jnp.mean(token_values, axis=1, keepdims=True)
    centred = token_values - average
    variance = jnp.mean(centred * centred, axis=1, keepdims=True)
    modulated = (
        (1.0 + modulation[1]) * (centred * lax.rsqrt(variance + 1e-06)) + modulation[0]
    ).astype(jnp.bfloat16)
    local_inner = qkv_weight.shape[2]
    head_dim = q_gain.shape[0]
    local_heads = local_inner // head_dim
    shard_rows = lax.all_gather(qkv_weight, "lon", axis=0, tiled=True)
    row_total = shard_rows.shape[0]
    projected = jnp.dot(
        modulated,
        shard_rows.reshape(row_total, 3 * local_inner),
        preferred_element_type=jnp.float32,
    )
    projected = projected.reshape(token_count, 3, local_inner) + qkv_bias.astype(jnp.float32)
    queries = rms_scale(
        projected[:, 0].reshape(lat_rows, col_count, local_heads, head_dim), q_gain
    ).astype(jnp.bfloat16)
    keys_normed = rms_scale(
        projected[:, 1].reshape(lat_rows, col_count, local_heads, head_dim), k_gain
    ).astype(jnp.bfloat16)
    values_image = projected[:, 2].astype(jnp.bfloat16).reshape(lat_rows, col_count, local_inner)
    key_value = jnp.stack(
        [keys_normed.reshape(lat_rows, col_count, local_inner), values_image], axis=2
    )
    widened = padded_2(key_value, (("lon", 1),), RADIUS)
    padded = jnp.pad(widened, ((RADIUS, RADIUS), (0, 0), (0, 0), (0, 0)))
    text_panel = lax.all_gather(text_kv, "lon", axis=1, tiled=True)
    text_count = text_panel.shape[1]
    text_keys = text_panel[0].reshape(text_count, local_heads, head_dim)
    text_values = text_panel[1].reshape(text_count, local_heads, head_dim)
    key_cols = col_count + 2 * RADIUS

    def one_block(block_index):
        row_first = block_index * QROWS
        query_block = lax.dynamic_slice_in_dim(queries, row_first, QROWS, 0)
        pair_block = lax.dynamic_slice_in_dim(padded, row_first, QROWS + 2 * RADIUS, 0)
        key_block = pair_block[:, :, 0].reshape(QROWS + 2 * RADIUS, key_cols, local_heads, head_dim)
        value_block = pair_block[:, :, 1].reshape(
            QROWS + 2 * RADIUS, key_cols, local_heads, head_dim
        )
        return attend(
            query_block, key_block, value_block, text_keys, text_values, row_first, lat_rows
        )

    attended = lax.map(one_block, jnp.arange(lat_rows // QROWS, dtype=jnp.int32)).reshape(
        token_count, local_inner
    )
    out_cols = model_width // head_groups
    col_offset = lax.axis_index("head") * out_cols
    proj_columns = lax.all_gather(proj_weight, "lon", axis=0, tiled=True)
    own_rows = lax.all_to_all(proj_columns, "head", split_axis=0, concat_axis=1, tiled=True)
    partial_out = jnp.dot(attended, own_rows, preferred_element_type=jnp.float32)
    out_sum = lax.psum_scatter(partial_out, "head", scatter_dimension=1, tiled=True)
    own_image = lax.dynamic_slice_in_dim(
        image_tokens.reshape(token_count, model_width), col_offset, out_cols, 1
    ).astype(jnp.float32)
    own_gate = lax.dynamic_slice_in_dim(modulation[2], col_offset, out_cols, 0)
    own_bias = lax.dynamic_slice_in_dim(proj_bias, col_offset, out_cols, 0).astype(jnp.float32)
    block_output = (own_image + own_gate * (out_sum + own_bias)).astype(jnp.bfloat16)
    return block_output.reshape(lat_rows, col_count, out_cols)


def solution(mesh):
    placed = (
        P(None, "lon", None),
        P(),
        P(("lon", "head"), None, None),
        P(),
        P("lon", None, "head"),
        P(None, "head"),
        P(),
        P(),
        P(None, "lon", "head"),
        P("lon", "head"),
        P(),
    )
    return jax.shard_map(
        body, mesh=mesh, in_specs=placed, out_specs=P(None, "lon", "head"), check_vma=False
    )
```

profile of v0, /device:TPU:0, one launch (start us, length us, event | category | flops | bytes accessed | tf_op | source)
XLA Modules:
  0.0 694.7 jit_solution(13399464902569084253)
XLA Ops:
  7.3 3.8 copy.79
  13.9 45.9 %psum.7 = f32[3,3072]{1,0:T(4,128)S(1)} all-reduce(f32[3,3072]{1,0:T(4,128)S(1)} %reshape.296), channel_id=1, replica_groups=mesh['lon'=8,'head'=4] {'lon','head'}, use_global_device_ids=true, to_apply=%region_0.1 | all-reduce | flops 9216 | bytes 73728 | tf_op jit(solution)/shard_map/psum | solution.py:108
  61.4 3.9 convert_reduce_fusion
  65.2 4.5 fusion.37
  69.9 7.3 %fusion.40 = bf16[64,16,3072]{2,1,0:T(8,128)(2,1)} fusion(bf16[64,16,3072]{2,1,0:T(8,128)(2,1)S(1)} %bitcast.76, f32[3072]{0:T(1024)S(1)} %bitcast.90, f32[64,16]{1,0:T(8,128)S(1)} %add_rsqrt_fusion.2, f32[64,16]{1,0:T(8,128)S(1)} %broadcast_multiply_fusion, f32[3072]{0:T(1024)S(1)} %bitcast.91), kind=kLoop, calls=%fused_computation.68 | loop fusion | flops 18874368 | bytes 12615680 | tf_op jit(solution)/shard_map/convert_element_type | solution.py:117
  77.2 5.0 all-to-all-start
  82.4 112.0 %all-gather.4.cloned.1.call-done = bf16[3072,3,768]{0,2,1:T(8,128)(2,1)} async-done(((bf16[384,3,768]{0,2,1:T(8,128)(2,1)}), bf16[3072,3,768]{0,2,1:T(8,128)(2,1)}) %all-gather.4.cloned.1.call-update) | async-done | bytes 14155792 | tf_op jit(solution)/shard_map/all_gather | solution.py:121
  194.4 19.7 %broadcast_add_fusion.1 = f32[1024,3,768]{2,0,1:T(8,128)S(1)} fusion(f32[3,768]{1,0:T(4,128)S(1)} %convert_element_type.84, bf16[1024,3072,1]{1,0,2:T(8,128)(2,1)} %bitcast.83, bf16[3072,3,768]{0,2,1:T(8,128)(2,1)} %all-gather.4.cloned.1.call-done), kind=kOutput, calls=%fused_computation.69 | convolution fusion | flops 14497873920 | bytes 29893632 | tf_op jit(solution)/shard_map/dot_general | solution.py:123
  214.1 4.1 fusion.51
  218.3 4.6 mul.153
  222.9 3.4 reduce_sum.64
  226.9 2.6 mul.154
  229.5 4.7 mul.155
  234.3 3.6 multiply_convert_fusion.1
  239.3 2.6 copy.82
  242.2 2.7 copy.83
  244.9 3.7 collective-permute-start.1
  248.6 5.6 fusion.52
  254.2 4.6 copy.96
  258.8 2.3 copy.92
  261.1 4.7 copy.97
  265.7 2.4 copy.93
  268.1 6.7 copy.94
  274.8 4.6 reshape_squeeze.13
  279.3 4.2 multiply_reduce_fusion.1
  285.9 2.9 multiply_convert_fusion
  290.2 18.0 %collective-permute-done = bf16[64,15,2,768]{3,0,2,1:T(8,128)(2,1)} collective-permute-done((bf16[64,15,2,768]{3,0,2,1:T(8,128)(2,1)}, bf16[64,15,2,768]{3,0,2,1:T(8,128)(2,1)}, u32[]{:S(2)}, u32[]{:S(2)}) %collective-permute-start) | collective-permute-done | bytes 2949152 | tf_op jit(solution)/shard_map/ppermute | solution.py:18
  308.2 3.5 copy.84
  311.7 3.5 copy.85
  315.2 18.1 %select_maximum_fusion = bf16[94,46,2,768]{3,1,0,2:T(8,128)(2,1)} fusion(bf16[64,15,2,768]{3,1,0,2:T(8,128)(2,1)S(1)} %copy.85, bf16[64,15,2,768]{3,1,0,2:T(8,128)(2,1)S(1)} %copy.84, bf16[64,16,1,768]{3,1,0,2:T(8,128)(2,1)S(1)} %bitcast.80, bf16[64,16,1,768]{3,1,0,2:T(8,128)(2,1)S(1)} %multiply_convert_fusion.1), kind=kLoop, calls=%fused_computation.60 | loop fusion | flops 99624960 | bytes 22327296 | tf_op jit(solution)/shard_map/concatenate | solution.py:16
  333.3 221.7 %while.13 = (s32[]{:T(128)}, bf16[4,16,16,768]{3,2,1,0:T(8,128)(2,1)}, s32[4]{0:T(128)S(1)}, bf16[94,46,2,768]{3,1,0,2:T(8,128)(2,1)}, bf16[64,16,6,128]{3,1,0,2...) while((s32[]{:T(128)}, ...), condition=%wide.region_10.11_spmd, body=%wide.region_5.10_spmd.sunk | while | flops 2117607168 | bytes 124344392 | solution.py:159
  334.8 5.1 constant_dynamic-slice_fusion.6
  339.9 7.7 %squeeze.25 = bf16[2116,6,128]{2,1,0:T(8,128)(2,1)} reshape(bf16[46,46,1,768]{3,1,0,2:T(8,128)(2,1)} %get-tuple-element.266) | data formatting | bytes 6500352 | tf_op jit(solution)/shard_map/while/body/eval_jaxpr/reshape;while/body/eval_jaxpr/reshape;while/body/eval_jaxpr/squeeze | solution.py:50
  348.7 2.0 fusion.81
  350.6 9.4 %fusion.82 = (f32[6,256]{1,0:T(8,128)S(1)}, f32[6,256,2116]{1,2,0:T(8,128)}) fusion(pred[256,2116]{0,1:T(8,128)(4,1)S(1)} %fusion.81, bf16[256,6,128]{2,0,1:T(8,128)(2,1)S(1)} %bitcast.77, bf16[2116,6,128]{2,1,0:T(8,128)(2,1)} %squeeze.25), kind=kOutput, calls=%fused_computation.3.clone.1 | convolution fusion | flops 841794048 | bytes 17191936 | tf_op jit(solution)/shard_map/while/body/eval_jaxpr/qhd,khd->hqk/dot_general | solution.py:54
  363.3 7.4 %fusion.83 = f32[6,256]{1,0:T(8,128)S(1)} fusion(f32[6,256,2116]{1,2,0:T(8,128)} %get-tuple-element.267, f32[6,256]{1,0:T(8,128)S(1)} %max.13, pred[256,2116]{0,1:T(8,128)(4,1)S(1)} %fusion.81), kind=kLoop, calls=%fused_computation.4.clone.1 | loop fusion | flops 12999168 | bytes 13554688 | tf_op jit(solution)/shard_map/while/body/eval_jaxpr/reduce_sum | solution.py:68
  370.8 5.0 squeeze.26
  375.7 10.1 %fusion.85 = f32[256,6,128]{0,2,1:T(8,128)S(1)} fusion(f32[6,256,2116]{1,2,0:T(8,128)} %get-tuple-element.267, f32[6,256]{1,0:T(8,128)S(1)} %add.300, f32[6,256]{1,0:T(8,128)S(1)} %max.13, pred[256,2116]{0,1:T(8,128)(4,1)} %copy-done.4, bf16[2116,6,128]{2,1,0:T(8,128)(2,1)} %squeeze.26), kind=kOutput, calls=%fused_computation.19.clone.1 | convolution fusion | flops 848295936 | bytes 17591296 | tf_op jit(solution)/shard_map/while/body/eval_jaxpr/hqk,khd->qhd/dot_general | solution.py:73
  390.2 5.1 constant_dynamic-slice_fusion.6
  395.3 7.7 %squeeze.25 = bf16[2116,6,128]{2,1,0:T(8,128)(2,1)} reshape(bf16[46,46,1,768]{3,1,0,2:T(8,128)(2,1)} %get-tuple-element.266) | data formatting | bytes 6500352 | tf_op jit(solution)/shard_map/while/body/eval_jaxpr/reshape;while/body/eval_jaxpr/reshape;while/body/eval_jaxpr/squeeze | solution.py:50
  404.0 2.0 fusion.81
  406.0 9.4 %fusion.82 = (f32[6,256]{1,0:T(8,128)S(1)}, f32[6,256,2116]{1,2,0:T(8,128)}) fusion(pred[256,2116]{0,1:T(8,128)(4,1)S(1)} %fusion.81, bf16[256,6,128]{2,0,1:T(8,128)(2,1)S(1)} %bitcast.77, bf16[2116,6,128]{2,1,0:T(8,128)(2,1)} %squeeze.25), kind=kOutput, calls=%fused_computation.3.clone.1 | convolution fusion | flops 841794048 | bytes 17191936 | tf_op jit(solution)/shard_map/while/body/eval_jaxpr/qhd,khd->hqk/dot_general | solution.py:54
  416.1 1.7 copy-done.2
  418.7 7.4 %fusion.83 = f32[6,256]{1,0:T(8,128)S(1)} fusion(f32[6,256,2116]{1,2,0:T(8,128)} %get-tuple-element.267, f32[6,256]{1,0:T(8,128)S(1)} %max.13, pred[256,2116]{0,1:T(8,128)(4,1)S(1)} %fusion.81), kind=kLoop, calls=%fused_computation.4.clone.1 | loop fusion | flops 12999168 | bytes 13554688 | tf_op jit(solution)/shard_map/while/body/eval_jaxpr/reduce_sum | solution.py:68
  426.1 5.0 squeeze.26
  431.1 10.1 %fusion.85 = f32[256,6,128]{0,2,1:T(8,128)S(1)} fusion(f32[6,256,2116]{1,2,0:T(8,128)} %get-tuple-element.267, f32[6,256]{1,0:T(8,128)S(1)} %add.300, f32[6,256]{1,0:T(8,128)S(1)} %max.13, pred[256,2116]{0,1:T(8,128)(4,1)} %copy-done.4, bf16[2116,6,128]{2,1,0:T(8,128)(2,1)} %squeeze.26), kind=kOutput, calls=%fused_computation.19.clone.1 | convolution fusion | flops 848295936 | bytes 17591296 | tf_op jit(solution)/shard_map/while/body/eval_jaxpr/hqk,khd->qhd/dot_general | solution.py:73
  445.6 5.1 constant_dynamic-slice_fusion.6
  450.7 7.7 %squeeze.25 = bf16[2116,6,128]{2,1,0:T(8,128)(2,1)} reshape(bf16[46,46,1,768]{3,1,0,2:T(8,128)(2,1)} %get-tuple-element.266) | data formatting | bytes 6500352 | tf_op jit(solution)/shard_map/while/body/eval_jaxpr/reshape;while/body/eval_jaxpr/reshape;while/body/eval_jaxpr/squeeze | solution.py:50
  459.4 2.0 fusion.81
  461.4 9.4 %fusion.82 = (f32[6,256]{1,0:T(8,128)S(1)}, f32[6,256,2116]{1,2,0:T(8,128)}) fusion(pred[256,2116]{0,1:T(8,128)(4,1)S(1)} %fusion.81, bf16[256,6,128]{2,0,1:T(8,128)(2,1)S(1)} %bitcast.77, bf16[2116,6,128]{2,1,0:T(8,128)(2,1)} %squeeze.25), kind=kOutput, calls=%fused_computation.3.clone.1 | convolution fusion | flops 841794048 | bytes 17191936 | tf_op jit(solution)/shard_map/while/body/eval_jaxpr/qhd,khd->hqk/dot_general | solution.py:54
  471.4 1.7 copy-done.2
  474.1 7.4 %fusion.83 = f32[6,256]{1,0:T(8,128)S(1)} fusion(f32[6,256,2116]{1,2,0:T(8,128)} %get-tuple-element.267, f32[6,256]{1,0:T(8,128)S(1)} %max.13, pred[256,2116]{0,1:T(8,128)(4,1)S(1)} %fusion.81), kind=kLoop, calls=%fused_computation.4.clone.1 | loop fusion | flops 12999168 | bytes 13554688 | tf_op jit(solution)/shard_map/while/body/eval_jaxpr/reduce_sum | solution.py:68
  481.5 5.0 squeeze.26
  486.5 10.1 %fusion.85 = f32[256,6,128]{0,2,1:T(8,128)S(1)} fusion(f32[6,256,2116]{1,2,0:T(8,128)} %get-tuple-element.267, f32[6,256]{1,0:T(8,128)S(1)} %add.300, f32[6,256]{1,0:T(8,128)S(1)} %max.13, pred[256,2116]{0,1:T(8,128)(4,1)} %copy-done.4, bf16[2116,6,128]{2,1,0:T(8,128)(2,1)} %squeeze.26), kind=kOutput, calls=%fused_computation.19.clone.1 | convolution fusion | flops 848295936 | bytes 17591296 | tf_op jit(solution)/shard_map/while/body/eval_jaxpr/hqk,khd->qhd/dot_general | solution.py:73
  500.9 5.1 constant_dynamic-slice_fusion.6
  506.1 7.7 %squeeze.25 = bf16[2116,6,128]{2,1,0:T(8,128)(2,1)} reshape(bf16[46,46,1,768]{3,1,0,2:T(8,128)(2,1)} %get-tuple-element.266) | data formatting | bytes 6500352 | tf_op jit(solution)/shard_map/while/body/eval_jaxpr/reshape;while/body/eval_jaxpr/reshape;while/body/eval_jaxpr/squeeze | solution.py:50
  514.8 2.0 fusion.81
  516.8 9.4 %fusion.82 = (f32[6,256]{1,0:T(8,128)S(1)}, f32[6,256,2116]{1,2,0:T(8,128)}) fusion(pred[256,2116]{0,1:T(8,128)(4,1)S(1)} %fusion.81, bf16[256,6,128]{2,0,1:T(8,128)(2,1)S(1)} %bitcast.77, bf16[2116,6,128]{2,1,0:T(8,128)(2,1)} %squeeze.25), kind=kOutput, calls=%fused_computation.3.clone.1 | convolution fusion | flops 841794048 | bytes 17191936 | tf_op jit(solution)/shard_map/while/body/eval_jaxpr/qhd,khd->hqk/dot_general | solution.py:54
  529.5 7.4 %fusion.83 = f32[6,256]{1,0:T(8,128)S(1)} fusion(f32[6,256,2116]{1,2,0:T(8,128)} %get-tuple-element.267, f32[6,256]{1,0:T(8,128)S(1)} %max.13, pred[256,2116]{0,1:T(8,128)(4,1)S(1)} %fusion.81), kind=kLoop, calls=%fused_computation.4.clone.1 | loop fusion | flops 12999168 | bytes 13554688 | tf_op jit(solution)/shard_map/while/body/eval_jaxpr/reduce_sum | solution.py:68
  536.9 5.0 squeeze.26
  541.9 10.1 %fusion.85 = f32[256,6,128]{0,2,1:T(8,128)S(1)} fusion(f32[6,256,2116]{1,2,0:T(8,128)} %get-tuple-element.267, f32[6,256]{1,0:T(8,128)S(1)} %add.300, f32[6,256]{1,0:T(8,128)S(1)} %max.13, pred[256,2116]{0,1:T(8,128)(4,1)} %copy-done.4, bf16[2116,6,128]{2,1,0:T(8,128)(2,1)} %squeeze.26), kind=kOutput, calls=%fused_computation.19.clone.1 | convolution fusion | flops 848295936 | bytes 17591296 | tf_op jit(solution)/shard_map/while/body/eval_jaxpr/hqk,khd->qhd/dot_general | solution.py:73
  555.0 10.2 %fusion.54 = f32[1024,3072]{1,0:T(8,128)} fusion(bf16[1024,768]{1,0:T(8,128)(2,1)} %bitcast.92, bf16[768,3072]{0,1:T(8,128)(2,1)} %bitcast.85), kind=kOutput, calls=%fused_computation.99 | convolution fusion | flops 4831838208 | bytes 18874368 | tf_op jit(solution)/shard_map/dot_general | solution.py:166
  566.7 117.4 %reduce-scatter.2.cloned.1.call-done = f32[1024,768]{1,0:T(8,128)} async-done(((f32[1024,3072]{1,0:T(8,128)}), f32[1024,768]{1,0:T(8,128)}) %reduce-scatter.2.cloned.1.call-update) | async-done | bytes 3145744 | tf_op jit(solution)/shard_map/reduce_scatter | solution.py:167
  684.0 4.0 add_convert_fusion
  (143 shorter events, 41.7 us)
Async XLA Ops:
  6.5 63.3 %copy-start = (f32[128]{0:T(128)S(1)}, f32[128]{0:T(128)}, u32[]{:S(2)}) copy-start(f32[128]{0:T(128)} %param.20) | copy-start | bytes 1540
  6.5 4.7 copy-start.8
  6.5 5.6 copy-start.6
  6.5 70.6 %all-gather.8.cloned.1.call-start = ((), (), s32[]{:S(2)}) async-start(), calls=%async_computation.4 | async-start | bytes 5308416 | tf_op jit(solution)/shard_map/all_gather | solution.py:164
  7.3 187.1 %all-gather.4.cloned.1.call-start = ((), (), s32[]{:S(2)}) async-start(), calls=%async_computation.2 | async-start | bytes 15925248 | tf_op jit(solution)/shard_map/all_gather | solution.py:121
  11.2 237.4 %all-gather.6.cloned.1.call-start = ((), (), s32[]{:S(2)}) async-start(), calls=%async_computation.3 | async-start | bytes 1769472 | tf_op jit(solution)/shard_map/all_gather | solution.py:141
  59.8 10.1 %slice-start = ((s8[6291456]{0:T(1024)(128)(4,1)}), s8[4194304]{0:T(1024)(128)(4,1)S(1)}, s32[]{:S(2)}) async-start(s8[6291456]{0:T(1024)(128)(4,1)} %bitcast.75), calls=%async_computation.6 | async-start | bytes 8388608
  61.4 8.5 %slice-start.1 = ((s8[6291456]{0:T(1024)(128)(4,1)}), s8[2097152]{0:T(1024)(128)(4,1)S(1)}, s32[]{:S(2)}) async-start(s8[6291456]{0:T(1024)(128)(4,1)} %bitcast.75), calls=%async_computation.7 | async-start | bytes 4194304
  65.2 4.6 copy-start.9
  77.2 190.9 %all-to-all-start = ((bf16[4,768,768]{2,1,0:T(8,128)(2,1)}), bf16[4,768,768]{2,1,0:T(8,128)(2,1)}, u32[]{:S(2)}, u32[]{:S(2)}) async-start(bf16[4,768,768]{2,1,0:T(8,128)(2,1)} %bitcast.84), calls=%async_computation | async-start | bytes 9437184 | tf_op jit(solution)/shard_map/all_to_all | solution.py:165
  82.2 601.9 %reduce-scatter.2.cloned.1.call-start = ((), (), s32[]{:S(2)}) async-start(), calls=%async_computation.5 | async-start | bytes 15728640 | tf_op jit(solution)/shard_map/reduce_scatter | solution.py:167
  241.9 66.3 %collective-permute-start = (bf16[64,15,2,768]{3,0,2,1:T(8,128)(2,1)}, bf16[64,15,2,768]{3,0,2,1:T(8,128)(2,1)}, u32[]{:S(2)}, u32[]{:S(2)}) collective-permute-start(bf16[64,15,2,768]{3,0,2,1:T(8,128)(2,1)} %copy.82), channel_id=1, source_target_pairs={{0,4},{4,8},{8,12},{12,16},{16,20},{20,24},{24,28},{28,0},{1,5},{5... | collective-permute-start | bytes 8847368 | tf_op jit(solution)/shard_map/ppermute | solution.py:18
  244.9 66.8 %collective-permute-start.1 = (bf16[64,15,2,768]{3,0,2,1:T(8,128)(2,1)}, bf16[64,15,2,768]{3,0,2,1:T(8,128)(2,1)}, u32[]{:S(2)}, u32[]{:S(2)}) collective-permute-start(bf16[64,15,2,768]{3,0,2,1:T(8,128)(2,1)} %copy.83), channel_id=1, source_target_pairs={{4,0},{8,4},{12,8},{16,12},{20,16},{24,20},{28,24},{0,28},{5,1},{9... | collective-permute-start | bytes 8847368 | tf_op jit(solution)/shard_map/ppermute | solution.py:20
  279.3 6.6 copy-start.10
  350.6 12.7 %copy-start.4 = (pred[256,2116]{0,1:T(8,128)(4,1)}, pred[256,2116]{0,1:T(8,128)(4,1)S(1)}, u32[]{:S(2)}) copy-start(pred[256,2116]{0,1:T(8,128)(4,1)S(1)} %fusion.81) | copy-start | bytes 1625092 | tf_op jit(solution)/shard_map/while
  350.6 9.4 %copy-start.5 = (bf16[512,6,128]{2,0,1:T(8,128)(2,1)S(1)}, bf16[512,6,128]{2,0,1:T(8,128)(2,1)}, u32[]{:S(2)}) copy-start(bf16[512,6,128]{2,0,1:T(8,128)(2,1)} %get-tuple-element.303) | copy-start | bytes 2359300 | tf_op jit(solution)/shard_map/while
  360.7 1.7 copy-start.2
  375.7 10.1 %copy-start.3 = (f32[6,256,512]{2,1,0:T(8,128)S(1)}, f32[6,256,512]{2,1,0:T(8,128)}, u32[]{:S(2)}) copy-start(f32[6,256,512]{2,1,0:T(8,128)} %copy-done.2) | copy-start | bytes 9437188 | tf_op jit(solution)/shard_map/while
  375.7 10.1 %copy-start.7 = (bf16[512,6,128]{2,0,1:T(8,128)(2,1)S(1)}, bf16[512,6,128]{2,0,1:T(8,128)(2,1)}, u32[]{:S(2)}) copy-start(bf16[512,6,128]{2,0,1:T(8,128)(2,1)} %get-tuple-element.304) | copy-start | bytes 2359300 | tf_op jit(solution)/shard_map/while
  406.0 12.7 %copy-start.4 = (pred[256,2116]{0,1:T(8,128)(4,1)}, pred[256,2116]{0,1:T(8,128)(4,1)S(1)}, u32[]{:S(2)}) copy-start(pred[256,2116]{0,1:T(8,128)(4,1)S(1)} %fusion.81) | copy-start | bytes 1625092 | tf_op jit(solution)/shard_map/while
  406.0 9.4 %copy-start.5 = (bf16[512,6,128]{2,0,1:T(8,128)(2,1)S(1)}, bf16[512,6,128]{2,0,1:T(8,128)(2,1)}, u32[]{:S(2)}) copy-start(bf16[512,6,128]{2,0,1:T(8,128)(2,1)} %get-tuple-element.303) | copy-start | bytes 2359300 | tf_op jit(solution)/shard_map/while
  416.0 1.7 copy-start.2
  431.1 10.1 %copy-start.3 = (f32[6,256,512]{2,1,0:T(8,128)S(1)}, f32[6,256,512]{2,1,0:T(8,128)}, u32[]{:S(2)}) copy-start(f32[6,256,512]{2,1,0:T(8,128)} %copy-done.2) | copy-start | bytes 9437188 | tf_op jit(solution)/shard_map/while
  431.1 10.1 %copy-start.7 = (bf16[512,6,128]{2,0,1:T(8,128)(2,1)S(1)}, bf16[512,6,128]{2,0,1:T(8,128)(2,1)}, u32[]{:S(2)}) copy-start(bf16[512,6,128]{2,0,1:T(8,128)(2,1)} %get-tuple-element.304) | copy-start | bytes 2359300 | tf_op jit(solution)/shard_map/while
  461.4 12.7 %copy-start.4 = (pred[256,2116]{0,1:T(8,128)(4,1)}, pred[256,2116]{0,1:T(8,128)(4,1)S(1)}, u32[]{:S(2)}) copy-start(pred[256,2116]{0,1:T(8,128)(4,1)S(1)} %fusion.81) | copy-start | bytes 1625092 | tf_op jit(solution)/shard_map/while
  461.4 9.4 %copy-start.5 = (bf16[512,6,128]{2,0,1:T(8,128)(2,1)S(1)}, bf16[512,6,128]{2,0,1:T(8,128)(2,1)}, u32[]{:S(2)}) copy-start(bf16[512,6,128]{2,0,1:T(8,128)(2,1)} %get-tuple-element.303) | copy-start | bytes 2359300 | tf_op jit(solution)/shard_map/while
  471.4 1.7 copy-start.2
  486.5 10.1 %copy-start.3 = (f32[6,256,512]{2,1,0:T(8,128)S(1)}, f32[6,256,512]{2,1,0:T(8,128)}, u32[]{:S(2)}) copy-start(f32[6,256,512]{2,1,0:T(8,128)} %copy-done.2) | copy-start | bytes 9437188 | tf_op jit(solution)/shard_map/while
  486.5 10.1 %copy-start.7 = (bf16[512,6,128]{2,0,1:T(8,128)(2,1)S(1)}, bf16[512,6,128]{2,0,1:T(8,128)(2,1)}, u32[]{:S(2)}) copy-start(bf16[512,6,128]{2,0,1:T(8,128)(2,1)} %get-tuple-element.304) | copy-start | bytes 2359300 | tf_op jit(solution)/shard_map/while
  516.8 12.7 %copy-start.4 = (pred[256,2116]{0,1:T(8,128)(4,1)}, pred[256,2116]{0,1:T(8,128)(4,1)S(1)}, u32[]{:S(2)}) copy-start(pred[256,2116]{0,1:T(8,128)(4,1)S(1)} %fusion.81) | copy-start | bytes 1625092 | tf_op jit(solution)/shard_map/while
  516.8 9.4 %copy-start.5 = (bf16[512,6,128]{2,0,1:T(8,128)(2,1)S(1)}, bf16[512,6,128]{2,0,1:T(8,128)(2,1)}, u32[]{:S(2)}) copy-start(bf16[512,6,128]{2,0,1:T(8,128)(2,1)} %get-tuple-element.303) | copy-start | bytes 2359300 | tf_op jit(solution)/shard_map/while
  526.8 1.7 copy-start.2
  541.9 10.1 %copy-start.3 = (f32[6,256,512]{2,1,0:T(8,128)S(1)}, f32[6,256,512]{2,1,0:T(8,128)}, u32[]{:S(2)}) copy-start(f32[6,256,512]{2,1,0:T(8,128)} %copy-done.2) | copy-start | bytes 9437188 | tf_op jit(solution)/shard_map/while
  541.9 10.1 %copy-start.7 = (bf16[512,6,128]{2,0,1:T(8,128)(2,1)S(1)}, bf16[512,6,128]{2,0,1:T(8,128)(2,1)}, u32[]{:S(2)}) copy-start(bf16[512,6,128]{2,0,1:T(8,128)(2,1)} %get-tuple-element.304) | copy-start | bytes 2359300 | tf_op jit(solution)/shard_map/while
  565.2 122.8 %copy-start.1 = (f32[128]{0:T(128)S(1)}, f32[128]{0:T(128)}, u32[]{:S(2)}) copy-start(f32[128]{0:T(128)} %param.20) | copy-start | bytes 1540
Sparse Core Ops, SparseCore 0:
  9.0 55.3 all-gather.7
  66.0 128.2 all-gather.3
  196.0 23.2 all-gather.5
  565.3 118.6 reduce-scatter.1
where the time goes:
time: 704 us; the launch traced here: 695 us
  waiting for transfers between devices  248 us (35%)
  local copies, waits for them, and re-layouts  156 us (22%)
  matrix products  118 us (17%)
  other arithmetic  101 us (14%)
  blocking collectives  45.9 us (7%)
  between operations  13.6 us (2%)
  starting transfers between devices  9.2 us (1%)
    reduce_scatter x1, waiting for transfers between devices, body(): lax.psum_scatter(partial_out, 'head', scatter_dimension=1, tiled=True)  117 us
    all_gather x1, waiting for transfers between devices, body(): shard_rows = lax.all_gather(qkv_weight, 'lon', axis=0, tiled=True)  112 us
    psum x1, blocking collectives, body(): lax.psum(partial_mod, ('lon', 'head')).reshape(3, model_width)  45.9 us
    dot_general x4, matrix products, attend(): jnp.einsum('hqk,khd->qhd', image_probs, flat_values, preferred_element_ty...  40.3 us
    dot_general x4, matrix products, attend(): jnp.einsum('qhd,khd->hqk', flat_query, flat_keys, preferred_element_type=...  37.5 us
    squeeze x4, local copies, waits for them, and re-layouts, attend(): flat_keys = key_block.reshape(k_rows * k_cols, heads_here, head_dim)  30.6 us
    reduce_sum x4, other arithmetic, attend(): jnp.sum(image_exp, axis=2, keepdims=True)  29.7 us
    slice x4, local copies, waits for them, and re-layouts, one_block(): pair_block[:, :, 1]  20.5 us
  transfers between devices with their start and end apart: 7, of which 3 were waited for; matrix products, arithmetic and copies ran while one was open for 17% of the time, Pallas kernels for 0%

commit v1 on v0

--- a/solution.py
+++ b/solution.py
@@ -6,6 +6,24 @@
 
 RADIUS = 15
 QROWS = 16
+
+
+def laid_out(blocks, dim):
+    dims = list(blocks.shape[1:])
+    dims[dim] *= blocks.shape[0]
+    return jnp.moveaxis(blocks, 0, dim).reshape(dims)
+
+
+def doubled(x, axis):
+    devices = lax.axis_size(axis)
+    pieces = x[None]
+    for level in range(devices.bit_length() - 1):
+        stride = 1 << level
+        theirs = lax.ppermute(pieces, axis, [(i, i ^ stride) for i in range(devices)])
+        both = jnp.stack([pieces, theirs])
+        upper = lax.axis_index(axis) >> level & 1
+        pieces = jnp.where(upper == 0, both, both[::-1]).reshape(-1, *x.shape)
+    return pieces
 
 
 def padded_2(cells, sides, width):
@@ -118,7 +136,7 @@
     local_inner = qkv_weight.shape[2]
     head_dim = q_gain.shape[0]
     local_heads = local_inner // head_dim
-    shard_rows = lax.all_gather(qkv_weight, "lon", axis=0, tiled=True)
+    shard_rows = laid_out(doubled(qkv_weight, "lon"), 0)
     row_total = shard_rows.shape[0]
     projected = jnp.dot(
         modulated,

time: 704 us -> 1080 us (1.53)
  blocking collectives: 45.9 us -> 334 us
  local copies, waits for them, and re-layouts: 156 us -> 204 us
  other arithmetic: 101 us -> 131 us
    psum x1, blocking collectives: 45.9 us -> 334 us  [body(): lax.psum(partial_mod, ('lon', 'head')).reshape(3, model_width)]
    ppermute x0 -> x3, waiting for transfers between devices: none -> 118 us  [doubled(): lax.ppermute(pieces, axis, [(i, i ^ stride) for i in range(devices)])]
    all_gather x1 -> x0, waiting for transfers between devices: 112 us -> none  [body(): shard_rows = lax.all_gather(qkv_weight, 'lon', axis=0, tiled=True)]
    another operation x0 -> x2, local copies, waits for them, and re-layouts: none -> 37.4 us  [the longest x1 23.4 us: body(): shard_rows.reshape(row_total, 3 * local_inner)]
    another operation x0 -> x4, other arithmetic: none -> 18.4 us  [doubled(): both = jnp.stack([pieces, theirs])]
    reshape x0 -> x1, local copies, waits for them, and re-layouts: none -> 14.1 us  [doubled(): pieces = jnp.where(upper == 0, both, both[::-1]).reshape(-1, *x.shape)]
    select_n x0 -> x2, other arithmetic: none -> 13.1 us  [doubled(): pieces = jnp.where(upper == 0, both, both[::-1]).reshape(-1, *x.shape)]
  transfers between devices with their start and end apart: 7 -> 9, of which waited for: 3 -> 4; matrix products, arithmetic and copies ran while one was open for 17% -> 19% of each run, Pallas kernels for 0% -> 0%
where the time goes in v1:
time: 1080 us; the launch traced here: 1070 us
  blocking collectives  334 us (31%)
  waiting for transfers between devices  254 us (24%)
  local copies, waits for them, and re-layouts  204 us (19%)
  other arithmetic  131 us (12%)
  matrix products  118 us (11%)
  starting transfers between devices  15.4 us (1%)
  between operations  13.6 us (1%)
    psum x1, blocking collectives, body(): lax.psum(partial_mod, ('lon', 'head')).reshape(3, model_width)  334 us
    ppermute x3, waiting for transfers between devices, doubled(): lax.ppermute(pieces, axis, [(i, i ^ stride) for i in range(devices)])  118 us
    reduce_scatter x1, waiting for transfers between devices, body(): lax.psum_scatter(partial_out, 'head', scatter_dimension=1, tiled=True)  118 us
    dot_general x4, matrix products, attend(): jnp.einsum('hqk,khd->qhd', image_probs, flat_values, preferred_element_ty...  40.1 us
    dot_general x4, matrix products, attend(): jnp.einsum('qhd,khd->hqk', flat_query, flat_keys, preferred_element_type=...  37.5 us
    squeeze x4, local copies, waits for them, and re-layouts, attend(): flat_keys = key_block.reshape(k_rows * k_cols, heads_here, head_dim)  30.6 us
    reduce_sum x4, other arithmetic, attend(): jnp.sum(image_exp, axis=2, keepdims=True)  29.7 us
    another operation x1, local copies, waits for them, and re-layouts, body(): shard_rows.reshape(row_total, 3 * local_inner)  23.4 us
  transfers between devices with their start and end apart: 9, of which 4 were waited for; matrix products, arithmetic and copies ran while one was open for 19% of the time, Pallas kernels for 0%

profile of v1, /device:TPU:0, one launch (start us, length us, event | category | flops | bytes accessed | tf_op | source)
XLA Modules:
  0.0 1074.7 jit_solution(6133735337892858861)
XLA Ops:
  7.3 3.2 collective-permute-done
  12.3 2.7 fusion.40
  15.0 2.9 collective-permute-start.1
  17.9 115.1 %collective-permute-done.1 = bf16[2,384,3,768]{3,1,2,0:T(8,128)(2,1)} collective-permute-done((bf16[2,384,3,768]{3,1,2,0:T(8,128)(2,1)}, bf16[2,384,3,768]{3,1,2,0:T(8,128)(2,1)}, u32[]{:S(2)}, u32[]{:S(2)}) %collective-permute-start.1) | collective-permute-done | bytes 3538976 | tf_op jit(solution)/shard_map/ppermute | solution.py:22
  133.0 2.6 pad_maximum_fusion.1
  135.7 4.3 reverse_select_fusion.1
  139.9 14.1 %copy.83 = bf16[4,384,3,768]{1,0,3,2:T(4,128)(2,1)} copy(bf16[4,384,3,768]{3,1,2,0:T(8,128)(2,1)} %bitcast.85) | data formatting | bytes 14155776 | tf_op jit(solution)/shard_map/reshape | solution.py:25
  154.0 2.8 collective-permute-start.2
  161.6 334.1 %psum.7 = f32[3,3072]{1,0:T(4,128)S(1)} all-reduce(f32[3,3072]{1,0:T(4,128)S(1)} %reshape.299), channel_id=1, replica_groups=mesh['lon'=8,'head'=4] {'lon','head'}, use_global_device_ids=true, to_apply=%region_0.1 | all-reduce | flops 9216 | bytes 73728 | tf_op jit(solution)/shard_map/psum | solution.py:126
  495.7 3.8 convert_reduce_fusion
  499.6 4.5 fusion.35
  504.8 6.5 fusion.38
  511.4 13.9 %copy.84 = bf16[1,4,384,3,768]{2,1,0,4,3:T(4,128)(2,1)} copy(bf16[1,4,384,3,768]{4,2,3,1,0:T(8,128)(2,1)} %bitcast.86) | data formatting | bytes 14155776 | tf_op jit(solution)/shard_map/stack;reshape | solution.py:23
  525.3 5.0 all-to-all-start
  530.5 11.2 %pad_maximum_fusion = bf16[2,4,384,3,768]{2,1,0,4,3:T(4,128)(2,1)S(1)} fusion(bf16[1,4,384,3,768]{2,1,0,4,3:T(4,128)(2,1)} %bitcast.19, bf16[1,4,384,3,768]{2,1,0,4,3:T(4,128)(2,1)} %copy.84), kind=kLoop, calls=%fused_computation.59 | loop fusion | flops 7077888 | bytes 28311552 | tf_op jit(solution)/shard_map/stack | solution.py:23
  541.8 8.8 reverse_select_fusion
  550.6 23.4 %reshape_reshape_reshape.3 = bf16[3072,2304]{0,1:T(8,128)(2,1)} reshape(bf16[2,4,384,3,768]{2,1,0,4,3:T(4,128)(2,1)} %reverse_select_fusion) | data formatting | bytes 28311552 | tf_op jit(solution)/shard_map/reshape;reshape;reshape | solution.py:143
  574.1 19.7 %broadcast_add_fusion.1 = f32[1024,3,768]{2,0,1:T(8,128)S(1)} fusion(f32[3,768]{1,0:T(4,128)S(1)} %convert_element_type.84, bf16[1024,3072,1]{1,0,2:T(8,128)(2,1)} %bitcast.94, bf16[3,768,3072]{2,1,0:T(8,128)(2,1)} %bitcast.91), kind=kOutput, calls=%fused_computation.72 | convolution fusion | flops 14497873920 | bytes 29893632 | tf_op jit(solution)/shard_map/dot_general | solution.py:141
  593.8 3.9 fusion.49
  597.9 4.6 mul.153
  602.5 3.4 reduce_sum.64
  609.0 4.9 mul.155
  613.9 3.6 multiply_convert_fusion.1
  618.9 2.7 copy.87
  624.7 3.5 collective-permute-start.4
  628.3 5.6 fusion.50
  633.9 4.7 copy.101
  640.9 4.7 copy.102
  647.8 6.6 copy.99
  654.4 4.6 reshape_squeeze.13
  659.0 4.2 multiply_reduce_fusion.1
  665.6 2.9 multiply_convert_fusion
  669.9 17.9 %collective-permute-done.3 = bf16[64,15,2,768]{3,0,2,1:T(8,128)(2,1)} collective-permute-done((bf16[64,15,2,768]{3,0,2,1:T(8,128)(2,1)}, bf16[64,15,2,768]{3,0,2,1:T(8,128)(2,1)}, u32[]{:S(2)}, u32[]{:S(2)}) %collective-permute-start.3) | collective-permute-done | bytes 2949152 | tf_op jit(solution)/shard_map/ppermute | solution.py:36
  687.8 3.5 copy.89
  691.3 3.5 copy.90
  694.8 18.1 %select_maximum_fusion = bf16[94,46,2,768]{3,1,0,2:T(8,128)(2,1)} fusion(bf16[64,15,2,768]{3,1,0,2:T(8,128)(2,1)S(1)} %copy.90, bf16[64,15,2,768]{3,1,0,2:T(8,128)(2,1)S(1)} %copy.89, bf16[64,16,1,768]{3,1,0,2:T(8,128)(2,1)S(1)} %bitcast.90, bf16[64,16,1,768]{3,1,0,2:T(8,128)(2,1)S(1)} %multiply_convert_fusion.1), kind=kLoop, calls=%fused_computation.60 | loop fusion | flops 99624960 | bytes 22327296 | tf_op jit(solution)/shard_map/concatenate | solution.py:34
  712.9 221.5 %while.13 = (s32[]{:T(128)}, bf16[4,16,16,768]{3,2,1,0:T(8,128)(2,1)}, s32[4]{0:T(128)S(1)}, bf16[94,46,2,768]{3,1,0,2:T(8,128)(2,1)}, bf16[64,16,6,128]{3,1,0,2...) while((s32[]{:T(128)}, ...), condition=%wide.region_10.11_spmd, body=%wide.region_5.10_spmd.sunk | while | flops 2117607168 | bytes 124344392 | solution.py:177
  714.4 5.1 constant_dynamic-slice_fusion.6
  719.5 7.7 squeeze.25
  730.2 9.4 fusion.81
  742.9 7.4 fusion.82
  750.4 4.9 squeeze.26
  755.3 10.0 fusion.84
  769.7 5.1 constant_dynamic-slice_fusion.6
  774.9 7.7 squeeze.25
  785.6 9.4 fusion.81
  798.3 7.4 fusion.82
  805.7 4.9 squeeze.26
  810.6 10.0 fusion.84
  825.1 5.1 constant_dynamic-slice_fusion.6
  830.2 7.7 squeeze.25
  840.9 9.4 fusion.81
  853.6 7.4 fusion.82
  861.0 4.9 squeeze.26
  866.0 10.0 fusion.84
  880.4 5.1 constant_dynamic-slice_fusion.6
  885.5 7.7 squeeze.25
  896.3 9.4 fusion.81
  908.9 7.4 fusion.82
  916.4 4.9 squeeze.26
  921.3 10.0 fusion.84
  934.4 10.1 fusion.52
  946.0 118.0 %reduce-scatter.2.cloned.1.call-done = f32[1024,768]{1,0:T(8,128)} async-done(((f32[1024,3072]{1,0:T(8,128)}), f32[1024,768]{1,0:T(8,128)}) %reduce-scatter.2.cloned.1.call-update) | async-done | bytes 3145744 | tf_op jit(solution)/shard_map/reduce_scatter | solution.py:185
  1064.0 4.0 add_convert_fusion
  (156 shorter events, 65.8 us)
Async XLA Ops:
  6.5 489.1 %copy-start = (f32[128]{0:T(128)S(1)}, f32[128]{0:T(128)}, u32[]{:S(2)}) copy-start(f32[128]{0:T(128)} %param.20) | copy-start | bytes 1540
  6.5 518.7 %all-gather.5.cloned.1.call-start = ((), (), s32[]{:S(2)}) async-start(), calls=%async_computation.3 | async-start | bytes 5308416 | tf_op jit(solution)/shard_map/all_gather | solution.py:182
  6.5 4.0 collective-permute-start
  7.3 621.0 %all-gather.3.cloned.1.call-start = ((), (), s32[]{:S(2)}) async-start(), calls=%async_computation.2 | async-start | bytes 1769472 | tf_op jit(solution)/shard_map/all_gather | solution.py:159
  15.0 118.0 %collective-permute-start.1 = (bf16[2,384,3,768]{3,1,2,0:T(8,128)(2,1)}, bf16[2,384,3,768]{3,1,2,0:T(8,128)(2,1)}, u32[]{:S(2)}, u32[]{:S(2)}) collective-permute-start(bf16[2,384,3,768]{3,1,2,0:T(8,128)(2,1)} %get-tuple-element.203), channel_id=1, source_target_pairs={{0,8},{4,12},{8,0},{12,4},{16,24},{20,28},{24,16},{28,20},{1,9},{5... | collective-permute-start | bytes 10616840 | tf_op jit(solution)/shard_map/ppermute | solution.py:22
  139.9 16.8 %copy-start.8 = (bf16[2,64,768]{2,1,0:T(8,128)(2,1)S(1)}, bf16[2,64,768]{2,1,0:T(8,128)(2,1)}, u32[]{:S(2)}) copy-start(bf16[2,64,768]{2,1,0:T(8,128)(2,1)} %param.21) | copy-start | bytes 589828
  139.9 17.8 %copy-start.6 = (bf16[96,3,3072]{2,0,1:T(8,128)(2,1)S(1)}, bf16[96,3,3072]{2,0,1:T(8,128)(2,1)}, u32[]{:S(2)}) copy-start(bf16[96,3,3072]{2,0,1:T(8,128)(2,1)} %param.15) | copy-start | bytes 5308420
  154.0 7.6 copy-start.10
  154.0 376.5 %collective-permute-start.2 = (bf16[4,384,3,768]{1,0,3,2:T(4,128)(2,1)}, bf16[4,384,3,768]{1,0,3,2:T(4,128)(2,1)}, u32[]{:S(2)}, u32[]{:S(2)}) collective-permute-start(bf16[4,384,3,768]{1,0,3,2:T(4,128)(2,1)} %copy.83), channel_id=1, source_target_pairs={{0,16},{4,20},{8,24},{12,28},{16,0},{20,4},{24,8},{28,12},{1,17},{... | collective-permute-start | bytes 21233672 | tf_op jit(solution)/shard_map/ppermute | solution.py:22
  159.0 345.8 %slice-start = ((s8[6291456]{0:T(1024)(128)(4,1)}), s8[2097152]{0:T(1024)(128)(4,1)S(1)}, s32[]{:S(2)}) async-start(s8[6291456]{0:T(1024)(128)(4,1)} %bitcast.83), calls=%async_computation.5 | async-start | bytes 4194304
  495.7 9.1 slice-start.1
  499.5 4.6 copy-start.9
  525.3 122.5 %all-to-all-start = ((bf16[4,768,768]{2,1,0:T(8,128)(2,1)}), bf16[4,768,768]{2,1,0:T(8,128)(2,1)}, u32[]{:S(2)}, u32[]{:S(2)}) async-start(bf16[4,768,768]{2,1,0:T(8,128)(2,1)} %bitcast.95), calls=%async_computation | async-start | bytes 9437184 | tf_op jit(solution)/shard_map/all_to_all | solution.py:183
  530.3 533.8 %reduce-scatter.2.cloned.1.call-start = ((), (), s32[]{:S(2)}) async-start(), calls=%async_computation.4 | async-start | bytes 15728640 | tf_op jit(solution)/shard_map/reduce_scatter | solution.py:185
  621.7 66.2 %collective-permute-start.3 = (bf16[64,15,2,768]{3,0,2,1:T(8,128)(2,1)}, bf16[64,15,2,768]{3,0,2,1:T(8,128)(2,1)}, u32[]{:S(2)}, u32[]{:S(2)}) collective-permute-start(bf16[64,15,2,768]{3,0,2,1:T(8,128)(2,1)} %copy.87), channel_id=1, source_target_pairs={{0,4},{4,8},{8,12},{12,16},{16,20},{20,24},{24,28},{28,0},{1,5},{5... | collective-permute-start | bytes 8847368 | tf_op jit(solution)/shard_map/ppermute | solution.py:36
  624.7 66.5 %collective-permute-start.4 = (bf16[64,15,2,768]{3,0,2,1:T(8,128)(2,1)}, bf16[64,15,2,768]{3,0,2,1:T(8,128)(2,1)}, u32[]{:S(2)}, u32[]{:S(2)}) collective-permute-start(bf16[64,15,2,768]{3,0,2,1:T(8,128)(2,1)} %copy.88), channel_id=1, source_target_pairs={{4,0},{8,4},{12,8},{16,12},{20,16},{24,20},{28,24},{0,28},{5,1},{9... | collective-permute-start | bytes 8847368 | tf_op jit(solution)/shard_map/ppermute | solution.py:38
  659.0 6.6 copy-start.11
  730.2 12.7 %copy-start.4 = (pred[256,2116]{0,1:T(8,128)(4,1)}, pred[256,2116]{0,1:T(8,128)(4,1)S(1)}, u32[]{:S(2)}) copy-start(pred[256,2116]{0,1:T(8,128)(4,1)S(1)} %fusion.80) | copy-start | bytes 1625092 | tf_op jit(solution)/shard_map/while
  730.2 9.4 copy-start.5
  740.3 1.7 copy-start.2
  755.3 10.0 copy-start.3
  755.3 10.1 copy-start.7
  785.6 12.7 %copy-start.4 = (pred[256,2116]{0,1:T(8,128)(4,1)}, pred[256,2116]{0,1:T(8,128)(4,1)S(1)}, u32[]{:S(2)}) copy-start(pred[256,2116]{0,1:T(8,128)(4,1)S(1)} %fusion.80) | copy-start | bytes 1625092 | tf_op jit(solution)/shard_map/while
  785.6 9.4 copy-start.5
  795.6 1.7 copy-start.2
  810.6 10.0 copy-start.3
  810.6 10.1 copy-start.7
  840.9 12.7 %copy-start.4 = (pred[256,2116]{0,1:T(8,128)(4,1)}, pred[256,2116]{0,1:T(8,128)(4,1)S(1)}, u32[]{:S(2)}) copy-start(pred[256,2116]{0,1:T(8,128)(4,1)S(1)} %fusion.80) | copy-start | bytes 1625092 | tf_op jit(solution)/shard_map/while
  840.9 9.4 copy-start.5
  851.0 1.7 copy-start.2
  866.0 10.0 copy-start.3
  866.0 10.1 copy-start.7
  896.2 12.7 %copy-start.4 = (pred[256,2116]{0,1:T(8,128)(4,1)}, pred[256,2116]{0,1:T(8,128)(4,1)S(1)}, u32[]{:S(2)}) copy-start(pred[256,2116]{0,1:T(8,128)(4,1)S(1)} %fusion.80) | copy-start | bytes 1625092 | tf_op jit(solution)/shard_map/while
  896.3 9.4 copy-start.5
  906.3 1.7 copy-start.2
  921.3 10.0 copy-start.3
  921.3 10.1 copy-start.7
  944.5 123.5 %copy-start.1 = (f32[128]{0:T(128)S(1)}, f32[128]{0:T(128)}, u32[]{:S(2)}) copy-start(f32[128]{0:T(128)} %param.20) | copy-start | bytes 1540
Sparse Core Ops, SparseCore 0:
  9.0 86.8 all-gather.4
  157.8 172.8 all-gather.2
  944.7 119.3 reduce-scatter.1
